TPU v7x, 128 devices: a whole 4x4x4 slice. The times are simulated.
128 devices in a mesh: dp: 32 (over x, z_hi, y), tensor: 4 (over z_lo, core).
Axes of the slice: x: 4, y: 4, z: 4 (z_hi: 2, z_lo: 2; z = z_hi * 2 + z_lo), core: 2. Of those that a mesh axis runs over, the one named last changes fastest.
Arguments:
- activations: bfloat16 [8192, 8192], P('dp'), may hold values from -6 to 6
- out_grad: bfloat16 [8192, 2048], P('dp', 'tensor'), may hold values from -6 to 6
- weight: bfloat16 [8192, 2048], P(None, 'tensor'), may hold values from -0.0625 to 0.0625
- left_stats: float32 [8192, 2048], P('dp', 'tensor'), may hold values from -100 to 100, as said below
- right_stats: float32 [8192, 2048], P('dp', 'tensor'), may hold values from -100 to 100, as said below
Outputs:
- input_grad: bfloat16 [8192, 8192], P('dp', 'tensor')
- update: bfloat16 [8192, 2048], P('dp', 'tensor')
- left_new: float32 [8192, 2048], P('dp', 'tensor')
- right_new: float32 [8192, 2048], P('dp', 'tensor')
Inputs may be any that keep to these rules, and one draw needn't show every extreme that they name: `left_stats`: every 512 x 512 block at rows i * 512 and columns j * 512 is symmetric and positive definite. `right_stats`: every 512 x 512 block at rows i * 512 and columns j * 512 is symmetric and positive definite.
All inputs are finite; a program needn't handle non-finite values.
Results may differ from a plain program's by a relative error of at most 0.001.
Values may be sent and summed in bfloat16 or wider, within the bound.
No kernel may reach another device: no remote copies, remote signals or barrier semaphores. Data moves between devices by JAX's collectives and lax.ppermute only.
A program may use at most 128 MiB of HBM per device.

v0:
```python
import jax
import jax.numpy as jnp
from jax import lax
from jax.sharding import PartitionSpec as P

BLOCK = 512
ITERS = 10


decay_rate = 0.9


def from_partner(value, axis, apart):
    mask = 2**apart
    pairs = [(source, source ^ mask) for source in range(lax.axis_size(axis))]
    return lax.ppermute(value, axis, pairs)


def batch_product(form, first, second):
    return jnp.einsum(form, first, second, precision=lax.Precision.HIGHEST)


def inverse_root(matrix):
    identity = jnp.eye(matrix.shape[-1], dtype=matrix.dtype)
    frobenius = jnp.sqrt(jnp.sum(matrix * matrix, axis=(1, 2), keepdims=True))
    current = matrix / frobenius
    result = jnp.broadcast_to(identity, matrix.shape)
    for iteration in range(ITERS):
        factor = (5.0 * identity - current) / 4.0
        result = batch_product("bij,bjk->bik", result, factor)
        squared = batch_product("bij,bjk->bik", factor, factor)
        fourth = batch_product("bij,bjk->bik", squared, squared)
        current = batch_product("bij,bjk->bik", fourth, current)
    return result / jnp.sqrt(jnp.sqrt(frobenius))


def split_blocks(whole_rows):
    row_total, col_total = whole_rows.shape
    shaped = whole_rows.reshape(row_total // BLOCK, BLOCK, col_total // BLOCK, BLOCK)
    return shaped.transpose(0, 2, 1, 3).reshape(-1, BLOCK, BLOCK)


def join_blocks(blocks, row_total, col_total):
    shaped = blocks.reshape(row_total // BLOCK, col_total // BLOCK, BLOCK, BLOCK)
    return shaped.transpose(0, 2, 1, 3).reshape(row_total, col_total)


def shards(activations, out_grad, weight, left_stats, right_stats):
    rows_local, cols_local = left_stats.shape
    dp_index = lax.axis_index("dp")
    tokens = activations.shape[0] * lax.axis_size("dp")
    summed = lax.psum_scatter(
        lax.dot_general(
            activations, out_grad, (((0,), (0,)), ((), ())), preferred_element_type=jnp.float32
        ),
        "dp",
        scatter_dimension=0,
        tiled=True,
    )
    grad_rows = summed * tokens ** (-0.5)
    partial_terms = lax.dot_general(
        out_grad, weight, (((1,), (1,)), ((), ())), preferred_element_type=jnp.float32
    )
    input_grad = lax.psum_scatter(partial_terms, "tensor", scatter_dimension=1, tiled=True).astype(
        jnp.bfloat16
    )
    lower_half = dp_index % 2 == 0
    partner_pieces = from_partner((grad_rows, left_stats, right_stats), "dp", 0)

    def attach(own_part, peer_part):
        return jnp.where(
            lower_half,
            jnp.concatenate([own_part, peer_part], 0),
            jnp.concatenate([peer_part, own_part], 0),
        )

    grad_full = attach(grad_rows, partner_pieces[0])
    left_full = attach(left_stats, partner_pieces[1])
    right_full = attach(right_stats, partner_pieces[2])
    grad_blocks = split_blocks(grad_full)
    left_gram = (
        decay_rate * split_blocks(left_full)
        + batch_product("bik,bjk->bij", grad_blocks, grad_blocks) / BLOCK
    )
    right_gram = (
        decay_rate * split_blocks(right_full)
        + batch_product("bki,bkj->bij", grad_blocks, grad_blocks) / BLOCK
    )
    own_stat = jnp.where(lower_half, left_gram, right_gram)
    own_root = inverse_root(own_stat)
    partner_root = from_partner(own_root, "dp", 0)
    left_root = jnp.where(lower_half, own_root, partner_root)
    right_root = jnp.where(lower_half, partner_root, own_root)
    update = batch_product(
        "bij,bjk->bik", batch_product("bij,bjk->bik", left_root, grad_blocks), right_root
    )
    row_total = grad_full.shape[0]
    update_rows = join_blocks(update, row_total, cols_local)
    left_rows = join_blocks(left_gram, row_total, cols_local)
    right_rows = join_blocks(right_gram, row_total, cols_local)
    offset = dp_index % 2 * rows_local
    update_rows = lax.dynamic_slice_in_dim(update_rows, offset, rows_local, 0)
    left_rows = lax.dynamic_slice_in_dim(left_rows, offset, rows_local, 0)
    right_rows = lax.dynamic_slice_in_dim(right_rows, offset, rows_local, 0)
    return (input_grad, update_rows.astype(jnp.bfloat16), left_rows, right_rows)


def solution(mesh):
    placed = (
        P("dp", None),
        P("dp", "tensor"),
        P(None, "tensor"),
        P("dp", "tensor"),
        P("dp", "tensor"),
    )
    return jax.shard_map(
        shards,
        mesh=mesh,
        in_specs=placed,
        out_specs=(P("dp", "tensor"), P("dp", "tensor"), P("dp", "tensor"), P("dp", "tensor")),
        check_vma=False,
    )
```

profile of v0, /device:TPU:0, one launch (start us, length us, event | category | flops | bytes accessed | tf_op | source)
XLA Modules:
  0.0 372.5 jit_solution(685662508892365411)
XLA Ops:
  8.1 10.3 %fusion.171 = f32[8192,512]{1,0:T(8,128)} fusion(bf16[256,8192]{1,0:T(8,128)(2,1)} %param.5, bf16[256,512]{1,0:T(8,128)(2,1)S(1)} %copy-done), kind=kOutput, calls=%fused_computation.177 | convolution fusion | flops 2147483648 | bytes 21233664 | tf_op jit(solution)/shard_map/dot_general | solution.py:53
  18.5 9.0 %fusion.170 = f32[256,8192]{1,0:T(8,128)} fusion(bf16[256,512]{1,0:T(8,128)(2,1)S(1)} %copy-done, bf16[8192,512]{1,0:T(8,128)(2,1)} %param.7), kind=kOutput, calls=%fused_computation.176 | convolution fusion | flops 2147483648 | bytes 17039360 | tf_op jit(solution)/shard_map/dot_general | solution.py:61
  30.2 222.3 %reduce-scatter.5.cloned.1.call-done = f32[256,512]{1,0:T(8,128)} async-done(((f32[8192,512]{1,0:T(8,128)}), f32[256,512]{1,0:T(8,128)}) %reduce-scatter.5.cloned.1.call-update) | async-done | bytes 524304 | tf_op jit(solution)/shard_map/reduce_scatter | solution.py:52
  253.7 2.2 collective-permute-start
  256.7 6.2 %collective-permute-done.1 = f32[256,512]{1,0:T(8,128)S(1)} collective-permute-done((f32[256,512]{1,0:T(8,128)S(1)}, f32[256,512]{1,0:T(8,128)S(1)}, u32[]{:S(2)}, u32[]{:S(2)}) %collective-permute-start.1) | collective-permute-done | bytes 524320 | tf_op jit(solution)/shard_map/ppermute | solution.py:16
  262.9 3.3 fusion.14
  266.2 2.4 collective-permute-done
  268.6 4.3 %multiply_reduce_fusion = (f32[]{:T(128)}, f32[512,512]{1,0:T(8,128)S(1)}) fusion(f32[512,512]{1,0:T(8,128)S(1)} %fusion.14, pred[]{:T(512)S(6)} %eq.31, f32[256,512]{1,0:T(8,128)S(1)} %collective-permute-done.1, f32[256,512]{1,0:T(8,128)S(1)} %broadcast_multiply_fusion, f32[256,512]{1,0:T(8,128)} %param.8, f32[256,512]{1,0:T(8,128)} %collective-permute-done), kind=kOutput, calls=%fused_computation.37 | convolution fusion | flops 1613758464 | bytes 4194309 | tf_op jit(solution)/shard_map/bik,bjk->bij/dot_general | solution.py:20
  273.9 1.9 fusion.54
  280.7 1.9 fusion.50
  282.6 2.1 fusion.174
  286.5 1.9 fusion.46
  292.2 1.9 fusion.42
  295.9 2.3 fusion.179
  298.2 1.9 fusion.38
  303.8 1.9 fusion.34
  309.5 1.9 fusion.30
  311.4 2.0 fusion.184
  315.3 1.9 fusion.26
  320.9 1.9 fusion.22
  324.7 2.1 fusion.1
  326.8 1.9 fusion.52
  328.7 1.9 fusion.48
  330.6 1.9 fusion.44
  332.5 1.9 fusion.40
  334.4 1.9 fusion.36
  336.3 1.9 fusion.32
  338.3 2.2 fusion.28
  340.5 1.9 fusion.24
  344.4 2.7 convert_element_type.7
  349.8 9.3 %collective-permute-done.3 = f32[1,512,512]{2,1,0:T(8,128)S(1)} collective-permute-done((f32[1,512,512]{2,1,0:T(8,128)S(1)}, f32[1,512,512]{2,1,0:T(8,128)S(1)}, u32[]{:S(2)}, u32[]{:S(2)}) %collective-permute-start.3) | collective-permute-done | bytes 1048608 | tf_op jit(solution)/shard_map/ppermute | solution.py:16
  359.1 3.4 fusion.17
  (47 shorter events, 40.2 us)
Async XLA Ops:
  7.2 1.0 copy-start
  7.2 245.3 %reduce-scatter.5.cloned.1.call-start = ((), (), s32[]{:S(2)}) async-start(), calls=%async_computation.3 | async-start | bytes 17301504 | tf_op jit(solution)/shard_map/reduce_scatter | solution.py:52
  18.5 325.9 %reduce-scatter.3.cloned.1.call-start = ((), (), s32[]{:S(2)}) async-start(), calls=%async_computation.2 | async-start | bytes 10485760 | tf_op jit(solution)/shard_map/reduce_scatter | solution.py:64
  27.5 1.0 copy-start.5
  27.5 226.2 %copy-start.6 = (f32[256,512]{1,0:T(8,128)S(1)}, f32[256,512]{1,0:T(8,128)}, u32[]{:S(2)}) copy-start(f32[256,512]{1,0:T(8,128)} %param.8) | copy-start | bytes 1572868
  28.5 227.3 %collective-permute-start.2 = (f32[256,512]{1,0:T(8,128)S(1)}, f32[256,512]{1,0:T(8,128)S(1)}, u32[]{:S(2)}, u32[]{:S(2)}) collective-permute-start(f32[256,512]{1,0:T(8,128)S(1)} %copy-done.5), channel_id=1, source_target_pairs={{0,4},{4,0},{8,12},{12,8},{16,20},{20,16},{24,28},{28,24},{32,36},... | collective-permute-start | bytes 1572872 | tf_op jit(solution)/shard_map/ppermute | solution.py:16
  253.6 22.2 %copy-start.3 = (f32[256,512]{1,0:T(8,128)}, f32[256,512]{1,0:T(8,128)S(1)}, u32[]{:S(2)}) copy-start(f32[256,512]{1,0:T(8,128)S(1)} %broadcast_multiply_fusion) | copy-start | bytes 1572868
  253.6 9.3 %collective-permute-start.1 = (f32[256,512]{1,0:T(8,128)S(1)}, f32[256,512]{1,0:T(8,128)S(1)}, u32[]{:S(2)}, u32[]{:S(2)}) collective-permute-start(f32[256,512]{1,0:T(8,128)S(1)} %broadcast_multiply_fusion), channel_id=1, source_target_pairs={{0,4},{4,0},{8,12},{12,8},{16,20},{20,16},{24,28},{28,24},{32,36},... | collective-permute-start | bytes 1572872 | tf_op jit(solution)/shard_map/ppermute | solution.py:16
  253.7 14.9 %collective-permute-start = (f32[256,512]{1,0:T(8,128)S(1)}, f32[256,512]{1,0:T(8,128)}, u32[]{:S(2)}, u32[]{:S(2)}) collective-permute-start(f32[256,512]{1,0:T(8,128)S(1)} %copy-done.6), channel_id=1, source_target_pairs={{0,4},{4,0},{8,12},{12,8},{16,20},{20,16},{24,28},{28,24},{32,36},... | collective-permute-start | bytes 1572872 | tf_op jit(solution)/shard_map/ppermute | solution.py:16
  255.9 0.8 copy-start.7
  262.9 12.9 %copy-start.4 = (f32[256,512]{1,0:T(8,128)}, f32[256,512]{1,0:T(8,128)S(1)}, u32[]{:S(2)}) copy-start(f32[256,512]{1,0:T(8,128)S(1)} %collective-permute-done.1) | copy-start | bytes 1572868
  272.8 11.8 %copy-start.2 = (f32[512,512]{1,0:T(8,128)}, f32[512,512]{1,0:T(8,128)S(1)}, u32[]{:S(2)}) copy-start(f32[512,512]{1,0:T(8,128)S(1)} %get-tuple-element.5) | copy-start | bytes 3145732
  340.4 24.7 %copy-start.1 = (bf16[256,512]{1,0:T(8,128)(2,1)S(1)}, bf16[256,512]{1,0:T(8,128)(2,1)}, u32[]{:S(2)}) copy-start(bf16[256,512]{1,0:T(8,128)(2,1)} %param.6) | copy-start | bytes 786436
  344.2 14.9 %collective-permute-start.3 = (f32[1,512,512]{2,1,0:T(8,128)S(1)}, f32[1,512,512]{2,1,0:T(8,128)S(1)}, u32[]{:S(2)}, u32[]{:S(2)}) collective-permute-start(f32[1,512,512]{2,1,0:T(8,128)S(1)} %fusion), channel_id=1, source_target_pairs={{0,4},{4,0},{8,12},{12,8},{16,20},{20,16},{24,28},{28,24},{32,36},... | collective-permute-start | bytes 3145736 | tf_op jit(solution)/shard_map/ppermute | solution.py:16
Sparse Core Ops, SparseCore 0:
  18.6 233.8 reduce-scatter.4
  255.0 76.8 reduce-scatter.2
where the time goes:
time: 378 us; the launch traced here: 372 us
  waiting for transfers between devices  240 us (63%)
  matrix products  102 us (27%)
  between operations  15.7 us (4%)
  local copies, waits for them, and re-layouts  6.16 us (2%)
  starting transfers between devices  4.1 us (1%)
  other arithmetic  4.03 us (1%)
    reduce_scatter x1, waiting for transfers between devices, shards(): lax.psum_scatter(lax.dot_general(activations, out_grad, (((0,), (0,)), ((...  222 us
    dot_general x41, matrix products, batch_product(): return jnp.einsum(form, first, second, precision=lax.Precision.HIGHEST)  83 us
    ppermute x4, waiting for transfers between devices, from_partner(): return lax.ppermute(value, axis, pairs)  17.9 us
    dot_general x1, matrix products, shards(): lax.dot_general(activations, out_grad, (((0,), (0,)), ((), ())), preferre...  10.3 us
    dot_general x1, matrix products, shards(): lax.dot_general(out_grad, weight, (((1,), (1,)), ((), ())), preferred_ele...  8.98 us
  transfers between devices with their start and end apart: 6, of which 4 were waited for; matrix products, arithmetic and copies ran while one was open for 25% of the time, Pallas kernels for 0%

commit v1 on v0

v1 whole, which is shorter than its diff:
```python
import jax
import jax.numpy as jnp
from jax import lax
from jax.experimental import pallas as pl
from jax.experimental.pallas import tpu as pltpu
from jax.sharding import Mesh, PartitionSpec as P


BLOCK = 512
HALF = 256
ITERS = 10
DECAY = 0.9
F32 = jnp.float32
BF16 = jnp.bfloat16
AXES = ("x", "zh", "y", "zl", "c")
SIZES = (4, 2, 4, 2, 2)
VMEM_SPEC = pl.BlockSpec(memory_space=pltpu.VMEM)
SMEM_SPEC = pl.BlockSpec(memory_space=pltpu.SMEM)


def params(mib):
    return pltpu.CompilerParams(vmem_limit_bytes=mib << 20)


def linear(x, zh, y, zl, c):
    return (((x * 2 + zh) * 4 + y) * 2 + zl) * 2 + c


def exchange(value, target):
    pairs = []
    for x in range(4):
        for zh in range(2):
            for y in range(4):
                for zl in range(2):
                    for c in range(2):
                        to = target(x, zh, y, zl, c)
                        if to is not None:
                            pairs.append((linear(x, zh, y, zl, c), linear(*to)))
    return lax.ppermute(value, AXES, pairs)


def other_core(value):
    return exchange(value, lambda x, zh, y, zl, c: (x, zh, y, zl, 1 - c))


def across_y(value, mask):
    return exchange(value, lambda x, zh, y, zl, c: (x, zh, y ^ mask, zl, c))


def parts_of(value):
    high = value.astype(BF16)
    return high, (value - high.astype(F32)).astype(BF16)


def contract(first, second, dims):
    def one(a, b):
        return lax.dot_general(a, b, (dims, ((), ())), preferred_element_type=F32)

    return one(first[0], second[0]) + (one(first[0], second[1]) + one(first[1], second[0]))


def multiply(first, second):
    return contract(first, second, ((1,), (0,)))


def spread_kernel(flags, acts, grads, rows_out, cols_out):
    first = flags[0] == 0
    for i in range(2):
        start = i * BLOCK
        rows_out[0, :, i * HALF : (i + 1) * HALF] = jnp.where(
            first, acts[:, start : start + HALF], acts[:, start + HALF : start + BLOCK]
        )
    cols_out[0] = grads[...]


def spread(flags, acts, grads):
    shape = jax.ShapeDtypeStruct((8, 256, BLOCK), BF16)
    out_spec = pl.BlockSpec((1, 256, BLOCK), lambda i: (i, 0, 0))
    return pl.pallas_call(
        spread_kernel,
        grid=(8,),
        out_shape=[shape, shape],
        in_specs=[
            SMEM_SPEC,
            pl.BlockSpec((256, 1024), lambda i: (0, i)),
            pl.BlockSpec((256, BLOCK), lambda i: (0, 0)),
        ],
        out_specs=[out_spec, out_spec],
        compiler_params=params(56),
        cost_estimate=pl.CostEstimate(flops=0, bytes_accessed=8 << 20, transcendentals=0),
    )(flags, acts, grads)


def grad_kernel(flags, acts, own, other, *outs):
    core, y = flags[0], flags[1]
    same = (y % 2) == core
    upper = (y // 2) == 1
    for row in range(2):
        for take_own in (True, False):
            flip_high = jnp.where(upper, 1 - row, row)
            flip_low = jnp.where(same, 0 if take_own else 1, 1 if take_own else 0)
            value = lax.dot_general(
                acts[:, row * HALF : (row + 1) * HALF],
                (own if take_own else other)[...],
                (((0,), (0,)), ((), ())),
                preferred_element_type=F32,
            )
            for k in range(4):

                @pl.when(flip_high * 2 + flip_low == k)
                def _(k=k, value=value):
                    outs[k][...] = value


def grad_terms(flags, acts, own, other):
    return pl.pallas_call(
        grad_kernel,
        out_shape=[jax.ShapeDtypeStruct((HALF, BLOCK), F32)] * 4,
        in_specs=[SMEM_SPEC] + [VMEM_SPEC] * 3,
        out_specs=[VMEM_SPEC] * 4,
        compiler_params=params(24),
        cost_estimate=pl.CostEstimate(
            flops=2 * acts.shape[0] * BLOCK * 1024, bytes_accessed=8 << 20, transcendentals=0
        ),
    )(flags, acts, own, other)


def input_kernel(place, grads, weight, *rest):
    value = lax.dot_general(
        grads[...], weight[...], (((1,), (1,)), ((), ())), preferred_element_type=F32
    )
    if len(rest) == 2:
        value = value + rest[0][0]
        rest[1][...] = value
    else:
        rest[0][0] = value


def input_terms(place, grads, weight, added=None, which=None):
    tile = BLOCK
    pairs = 2 if which is None else 1
    base = 0 if which is None else which

    def rows(i, n, where):
        zl, core = where[0], where[1]
        zl = jnp.where(i + base == 0, zl, 1 - zl)
        return ((zl * 2 + core) * 4 + n, 0)

    in_specs = [
        pl.BlockSpec((256, BLOCK), lambda i, n, where: (0, 0)),
        pl.BlockSpec((tile, BLOCK), rows),
    ]
    operands = [grads, weight]
    if which is None:
        out_shape = jax.ShapeDtypeStruct((2, 256, 2048), F32)
        out_spec = pl.BlockSpec((1, 256, tile), lambda i, n, where: (i, 0, n))
    else:
        in_specs.append(pl.BlockSpec((1, 256, tile), lambda i, n, where: (which, 0, n)))
        operands.append(added)
        out_shape = jax.ShapeDtypeStruct((256, 2048), F32)
        out_spec = pl.BlockSpec((256, tile), lambda i, n, where: (0, n))
    return pl.pallas_call(
        input_kernel,
        out_shape=out_shape,
        grid_spec=pltpu.PrefetchScalarGridSpec(
            num_scalar_prefetch=1, grid=(pairs, 4), in_specs=in_specs, out_specs=out_spec
        ),
        compiler_params=params(56),
        cost_estimate=pl.CostEstimate(
            flops=pairs << 29, bytes_accessed=pairs << 22, transcendentals=0
        ),
    )(place, *operands)


def gram_kernel(flags, grad_own, grad_other, stat_self, stat_p1, stat_p2, stat_p3, grad, mine, opposite):
    core, low = flags[0], flags[1] % 2
    diagonal = core == low
    grad[pl.ds(pl.multiple_of(core * HALF, HALF), HALF), :] = grad_own[...]
    grad[pl.ds(pl.multiple_of((1 - core) * HALF, HALF), HALF), :] = grad_other[...]
    stat_mine = jnp.where(diagonal, stat_self[...], stat_p2[...])
    stat_opposite = jnp.where(diagonal, stat_p1[...], stat_p3[...])
    whole = parts_of(grad[...])

    def store(product):
        lower, upper = product[:HALF] * (1.0 / BLOCK), product[HALF:] * (1.0 / BLOCK)
        mine[...] = DECAY * stat_mine + jnp.where(low == 0, lower, upper)
        opposite[...] = DECAY * stat_opposite + jnp.where(low == 0, upper, lower)

    @pl.when(core == 0)
    def _():
        store(contract(whole, whole, ((1,), (1,))))

    @pl.when(core == 1)
    def _():
        store(contract(whole, whole, ((0,), (0,))))


def new_statistics(flags, grad_own, grad_other, stats):
    half = jax.ShapeDtypeStruct((HALF, BLOCK), F32)
    return pl.pallas_call(
        gram_kernel,
        out_shape=[jax.ShapeDtypeStruct((BLOCK, BLOCK), F32), half, half],
        in_specs=[SMEM_SPEC] + [VMEM_SPEC] * 6,
        out_specs=[VMEM_SPEC] * 3,
        compiler_params=params(20),
        cost_estimate=pl.CostEstimate(flops=6 * BLOCK**3, bytes_accessed=5 << 20, transcendentals=0),
    )(flags, grad_own, grad_other, *stats)


def quarters(values):
    s11, s12, s22 = (parts_of(v) for v in values)
    return s11, s12, parts_of(values[1].T), s22


def product(first, second):
    return (
        multiply(first[0], second[0]) + multiply(first[1], second[2]),
        multiply(first[0], second[1]) + multiply(first[1], second[3]),
        multiply(first[2], second[1]) + multiply(first[3], second[3]),
    )


def root_kernel(flags, mine, opposite, root, current, result):
    low = flags[1] % 2 == 0
    top = jnp.where(low, mine[...], opposite[...])
    bottom = jnp.where(low, opposite[...], mine[...])
    squares = top * top + bottom * bottom
    total = jnp.sum(jnp.sum(squares, axis=0, keepdims=True), axis=1, keepdims=True)
    frobenius = jnp.sqrt(total)
    inverse = 1.0 / frobenius
    rows = lax.broadcasted_iota(jnp.int32, (HALF, HALF), 0)
    unit = jnp.where(rows == lax.broadcasted_iota(jnp.int32, (HALF, HALF), 1), 1.25, 0.0)

    def load(ref):
        return [ref[0], ref[1], ref[2]]

    def store(ref, value):
        for j in range(3):
            ref[j] = value[j]

    def next_current(matrix, split):
        square = product(split, split)
        rest = quarters([square[j] * (1 / 16) - 0.625 * matrix[j] for j in range(3)])
        once = [1.5625 * matrix[j] + v for j, v in enumerate(product(rest, split))]
        twice = product(rest, quarters(once))
        store(current, [1.5625 * once[j] + twice[j] for j in range(3)])

    def next_result(split):
        value = load(result)
        moved = product(quarters(value), split)
        return [1.25 * value[j] - 0.25 * moved[j] for j in range(3)]

    store(current, [top[:, :HALF] * inverse, top[:, HALF:] * inverse, bottom[:, HALF:] * inverse])
    matrix = load(current)
    store(result, [unit - 0.25 * matrix[0], -0.25 * matrix[1], unit - 0.25 * matrix[2]])
    next_current(matrix, quarters(matrix))

    def step(_, carry):
        matrix = load(current)
        split = quarters(matrix)
        store(result, next_result(split))
        next_current(matrix, split)
        return carry

    lax.fori_loop(1, ITERS - 1, step, 0)
    value = next_result(quarters(load(current)))
    scale = 1.0 / jnp.sqrt(jnp.sqrt(frobenius))
    root[:HALF, :HALF] = value[0] * scale
    root[:HALF, HALF:] = value[1] * scale
    root[HALF:, :HALF] = value[1].T * scale
    root[HALF:, HALF:] = value[2] * scale


def inverse_root(flags, mine, opposite):
    return pl.pallas_call(
        root_kernel,
        out_shape=jax.ShapeDtypeStruct((BLOCK, BLOCK), F32),
        in_specs=[SMEM_SPEC] + [VMEM_SPEC] * 2,
        out_specs=VMEM_SPEC,
        scratch_shapes=[pltpu.VMEM((3, HALF, HALF), F32), pltpu.VMEM((3, HALF, HALF), F32)],
        compiler_params=params(20),
        cost_estimate=pl.CostEstimate(flops=200 * BLOCK**3, bytes_accessed=2 << 20, transcendentals=0),
    )(flags, mine, opposite)


def update_kernel(flags, own, peer, grad, out):
    core = flags[0]
    rows = pl.ds(pl.multiple_of(core * HALF, HALF), HALF)

    def store(left, right):
        first = multiply(parts_of(left), parts_of(grad[...]))
        out[...] = multiply(parts_of(first), parts_of(right)).astype(BF16)

    store(jnp.where(core == 0, own[rows, :], peer[rows, :]), jnp.where(core == 0, peer[...], own[...]))


def update_rows(flags, own, peer, grad):
    return pl.pallas_call(
        update_kernel,
        out_shape=jax.ShapeDtypeStruct((HALF, BLOCK), BF16),
        in_specs=[SMEM_SPEC] + [VMEM_SPEC] * 3,
        out_specs=VMEM_SPEC,
        compiler_params=params(20),
        cost_estimate=pl.CostEstimate(flops=6 * BLOCK**3, bytes_accessed=4 << 20, transcendentals=0),
    )(flags, own, peer, grad)


def body(activations, out_grad, weight, left_stats, right_stats):
    y, zl, core = lax.axis_index("y"), lax.axis_index("zl"), lax.axis_index("c")
    low = y % 2
    tokens = activations.shape[0] * 32
    flags = jnp.stack([core, y]).astype(jnp.int32)
    diagonal = core == low

    rows, cols = spread(flags, activations, out_grad)
    rows, cols, out_grad = lax.optimization_barrier((rows, cols, out_grad))
    own_cols = lax.all_to_all(cols, ("x", "zh"), 0, 0, tiled=True).reshape(-1, BLOCK)
    acts = lax.all_to_all(rows, ("x", "zh"), 0, 0, tiled=True).reshape(-1, BLOCK)
    other_cols = other_core(own_cols)

    own_kind = jnp.where(core == 0, left_stats, right_stats)
    other_kind = jnp.where(core == 0, right_stats, left_stats)
    stat_p1 = exchange(
        own_kind, lambda x, zh, y, zl, c: (x, zh, y ^ 1, zl, c) if y % 2 != c else None
    )
    stat_p2 = exchange(
        other_kind, lambda x, zh, y, zl, c: (x, zh, y, zl, 1 - c) if y % 2 == c else None
    )
    stat_p3 = exchange(
        other_kind, lambda x, zh, y, zl, c: (x, zh, y ^ 1, zl, 1 - c) if y % 2 != c else None
    )

    for_other = input_terms(jnp.stack([zl, 1 - core]).astype(jnp.int32), out_grad, weight)
    from_other = other_core(for_other)
    place = jnp.stack([zl, core]).astype(jnp.int32)
    sent = input_terms(place, out_grad, weight, from_other, 1)
    kept = input_terms(place, out_grad, weight, from_other, 0)

    acts, sent, kept, stat_p1, stat_p2, stat_p3 = lax.optimization_barrier(
        (acts, sent, kept, stat_p1, stat_p2, stat_p3)
    )
    came = exchange(sent, lambda x, zh, y, zl, c: (x, zh, y, 1 - zl, c))

    terms = grad_terms(flags, acts, own_cols, other_cols)
    arrived = [across_y(terms[k], k) for k in (1, 2, 3)]
    grad_half = (terms[0] + arrived[0] + arrived[1] + arrived[2]) * tokens ** (-0.5)
    grad, mine, opposite = new_statistics(
        flags, grad_half, other_core(grad_half), (own_kind, stat_p1, stat_p2, stat_p3)
    )
    out_p1 = exchange(
        opposite, lambda x, zh, y, zl, c: (x, zh, y ^ 1, zl, c) if y % 2 == c else None
    )
    out_p2 = exchange(mine, lambda x, zh, y, zl, c: (x, zh, y, zl, 1 - c) if y % 2 != c else None)
    out_p3 = exchange(
        opposite, lambda x, zh, y, zl, c: (x, zh, y ^ 1, zl, 1 - c) if y % 2 != c else None
    )
    root = inverse_root(flags, mine, opposite)
    update = update_rows(flags, root, other_core(root), grad)
    crossed = exchange(
        update, lambda x, zh, y, zl, c: (x, zh, y ^ 1, zl, 1 - c) if y % 2 != c else None
    )
    update = jnp.where(diagonal, update, crossed)
    left_rows = jnp.where(
        core == 0, jnp.where(low == 0, mine, out_p1), jnp.where(low == 0, out_p3, out_p2)
    )
    right_rows = jnp.where(
        core == 0, jnp.where(low == 0, out_p2, out_p3), jnp.where(low == 0, out_p1, mine)
    )
    input_grad = (kept + came).astype(BF16)
    return input_grad, update, left_rows, right_rows


def solution(mesh):
    wide = Mesh(mesh.devices.reshape(SIZES), AXES)
    dp, tensor = ("x", "zh", "y"), ("zl", "c")
    both = P(dp, tensor)
    return jax.shard_map(
        body,
        mesh=wide,
        in_specs=(P(dp, None), both, P(None, tensor), both, both),
        out_specs=(both, both, both, both),
        check_vma=False,
    )
```

time: 378 us -> 187 us (0.49)
  the two profiles are of different devices: /device:TPU:0 before, /device:TPU:1 now
where the time goes in v1:
time: 187 us; the launch traced here: 186 us
  Pallas kernels  63.4 us (34%)
  waiting for transfers between devices  43.9 us (23%)
  blocking collectives  35.2 us (19%)
  starting transfers between devices  31.9 us (17%)
  other arithmetic  9.45 us (5%)
    all_to_all x1, blocking collectives, body(): lax.all_to_all(cols, ('x', 'zh'), 0, 0, tiled=True).reshape(-1, BLOCK)  35.2 us
    ppermute x15, waiting for transfers between devices, exchange(): return lax.ppermute(value, AXES, pairs)  34.1 us
    ppermute x15, starting transfers between devices, exchange(): return lax.ppermute(value, AXES, pairs)  27.6 us
    pallas_call x1, Pallas kernels, inverse_root(): pl.pallas_call(root_kernel, out_shape=jax.ShapeDtypeStruct((BLOCK, BLOCK)...  26.6 us
    pallas_call x3, Pallas kernels, input_terms(): pl.pallas_call(input_kernel, out_shape=out_shape, grid_spec=pltpu.Prefetc...  20 us
    all_to_all x1, waiting for transfers between devices, body(): lax.all_to_all(rows, ('x', 'zh'), 0, 0, tiled=True).reshape(-1, BLOCK)  9.77 us
    pallas_call x1, Pallas kernels, spread(): pl.pallas_call(spread_kernel, grid=(8,), out_shape=[shape, shape], in_spe...  6.71 us
    pallas_call x1, Pallas kernels, grad_terms(): pl.pallas_call(grad_kernel, out_shape=[jax.ShapeDtypeStruct((HALF, BLOCK)...  5.32 us
  transfers between devices with their start and end apart: 16, of which 7 were waited for; matrix products, arithmetic and copies ran while one was open for 4% of the time, Pallas kernels for 23%

profile of v1, /device:TPU:1, one launch (start us, length us, event | category | flops | bytes accessed | tf_op | source)
XLA Modules:
  0.0 186.2 jit_solution(17975901451412822829)
XLA Ops:
  1.3 6.7 %shard_map.84 = (bf16[8,256,512]{2,1,0:T(8,128)(2,1)}, bf16[8,256,512]{2,1,0:T(8,128)(2,1)}) custom-call(s32[2]{0:T(128)} %pad_add_fusion.flags, bf16[256,8192]{1,0:T(8,128)(2,1)} %acts.1, bf16[256,512]{1,0:T(8,128)(2,1)} %grads.4), custom_call_target="tpu_custom_call" | custom-call | bytes 8388608 | tf_op jit(solution)/shard_map/pallas_call | solution.py:79
  8.5 8.6 %shard_map.85 = f32[2,256,2048]{2,1,0:T(8,128)} custom-call(s32[2]{0:T(128)} %pad_add_fusion.2.place, bf16[256,512]{1,0:T(8,128)(2,1)} %grads.4, bf16[8192,512]{1,0:T(8,128)(2,1)} %weight.5), custom_call_target="tpu_custom_call" | custom-call | flops 1073741824 | bytes 8388608 | tf_op jit(solution)/shard_map/pallas_call | solution.py:162
  17.2 1.4 collective-permute-start
  18.5 35.2 %all_to_all.10 = bf16[8,256,512]{2,1,0:T(8,128)(2,1)S(1)} all-to-all(bf16[8,256,512]{2,1,0:T(8,128)(2,1)S(1)} %copy-done.6), channel_id=1, replica_groups=mesh['x'=4,'zh'=2,'y'=4,'zl'=2,'c'=2] {'x','zh'}, dimensions={0} | all-to-all | bytes 4194304 | tf_op jit(solution)/shard_map/all_to_all | solution.py:317
  53.7 1.1 collective-permute-start.5
  54.8 4.4 %all-to-all-start = ((bf16[8,256,512]{2,1,0:T(8,128)(2,1)}), bf16[8,256,512]{2,1,0:T(8,128)(2,1)}, u32[]{:S(2)}, u32[]{:S(2)}) async-start(bf16[8,256,512]{2,1,0:T(8,128)(2,1)} %get-tuple-element.24), calls=%async_computation | async-start | bytes 4194304 | tf_op jit(solution)/shard_map/all_to_all | solution.py:318
  59.2 1.1 broadcast_select_fusion.1
  60.3 3.2 %collective-permute-start.1 = (f32[256,512]{1,0:T(8,128)S(1)}, f32[256,512]{1,0:T(8,128)S(1)}, u32[]{:S(2)}, u32[]{:S(2)}) collective-permute-start(f32[256,512]{1,0:T(8,128)S(1)} %get-tuple-element.43.stat_self), channel_id=1, source_target_pairs={{1,5},{3,7},{4,0},{6,2},{9,13},{11,15},{12,8},{14,10},{17,21},{19,... | collective-permute-start | bytes 1572872 | tf_op jit(solution)/shard_map/ppermute | solution.py:39
  63.6 1.3 collective-permute-start.2
  64.9 2.4 %collective-permute-start.3 = (f32[256,512]{1,0:T(8,128)S(1)}, f32[256,512]{1,0:T(8,128)S(1)}, u32[]{:S(2)}, u32[]{:S(2)}) collective-permute-start(f32[256,512]{1,0:T(8,128)S(1)} %get-tuple-element.42), channel_id=1, source_target_pairs={{1,4},{3,6},{4,1},{6,3},{9,12},{11,14},{12,9},{14,11},{17,20},{19,... | collective-permute-start | bytes 1572872 | tf_op jit(solution)/shard_map/ppermute | solution.py:39
  67.9 5.6 %shard_map.86 = f32[256,2048]{1,0:T(8,128)} custom-call(s32[2]{0:T(128)} %pad_add_fusion.1.place, bf16[256,512]{1,0:T(8,128)(2,1)} %grads.4, bf16[8192,512]{1,0:T(8,128)(2,1)} %weight.5, f32[2,256,2048]{2,1,0:T(8,128)} %collective-permute-done.rest_0_), custom_call_target="tpu_custom_call" | custom-call | flops 536870912 | bytes 4194304 | tf_op jit(solution)/shard_map/pallas_call | solution.py:162
  73.5 5.7 %shard_map.87 = f32[256,2048]{1,0:T(8,128)} custom-call(s32[2]{0:T(128)} %pad_add_fusion.1.place, bf16[256,512]{1,0:T(8,128)(2,1)} %grads.4, bf16[8192,512]{1,0:T(8,128)(2,1)} %weight.5, f32[2,256,2048]{2,1,0:T(8,128)} %collective-permute-done.rest_0_), custom_call_target="tpu_custom_call" | custom-call | flops 536870912 | bytes 4194304 | tf_op jit(solution)/shard_map/pallas_call | solution.py:162
  79.2 0.8 copy-done
  80.0 0.8 copy-done.2
  80.8 9.8 %all-to-all-done = bf16[8,256,512]{2,1,0:T(8,128)(2,1)} async-done(((bf16[8,256,512]{2,1,0:T(8,128)(2,1)}), bf16[8,256,512]{2,1,0:T(8,128)(2,1)}, u32[]{:S(2)}, u32[]{:S(2)}) %all-to-all-start) | async-done | bytes 2097184 | tf_op jit(solution)/shard_map/all_to_all | solution.py:318
  90.6 5.3 %shard_map.88 = (f32[256,512]{1,0:T(8,128)S(1)}, f32[256,512]{1,0:T(8,128)S(1)}, f32[256,512]{1,0:T(8,128)S(1)}, f32[256,512]{1,0:T(8,128)S(1)}) custom-call(s32[2]{0:T(128)S(1)} %copy-done.4, bf16[2048,512]{1,0:T(8,128)(2,1)} %bitcast.2.acts, bf16[2048,512]{1,0:T(8,128)(2,1)S(1)} %bitcast.7, bf16[2048,512]{1,0:T(8,128)(2,1)} %collective-permute-done.5.other), custom_call_target="tpu_custom_call" | custom-call | flops 2147483648 | bytes 8388608 | tf_op jit(solution)/shard_map/pallas_call | solution.py:116
  95.9 2.8 %collective-permute-start.8 = (f32[256,512]{1,0:T(8,128)S(1)}, f32[256,512]{1,0:T(8,128)S(1)}, u32[]{:S(2)}, u32[]{:S(2)}) collective-permute-start(f32[256,512]{1,0:T(8,128)S(1)} %get-tuple-element.33), channel_id=1, source_target_pairs={{0,12},{1,13},{2,14},{3,15},{4,8},{5,9},{6,10},{7,11},{8,4},{9,5},... | collective-permute-start | bytes 1572872 | tf_op jit(solution)/shard_map/ppermute | solution.py:39
  99.4 21.8 %collective-permute-done.8 = f32[256,512]{1,0:T(8,128)S(1)} collective-permute-done((f32[256,512]{1,0:T(8,128)S(1)}, f32[256,512]{1,0:T(8,128)S(1)}, u32[]{:S(2)}, u32[]{:S(2)}) %collective-permute-start.8) | collective-permute-done | bytes 524320 | tf_op jit(solution)/shard_map/ppermute | solution.py:39
  121.9 2.0 %collective-permute-start.9 = (f32[256,512]{1,0:T(8,128)S(1)}, f32[256,512]{1,0:T(8,128)S(1)}, u32[]{:S(2)}, u32[]{:S(2)}) collective-permute-start(f32[256,512]{1,0:T(8,128)S(1)} %add_multiply_fusion.grad_own), channel_id=1, source_target_pairs={{0,1},{1,0},{2,3},{3,2},{4,5},{5,4},{6,7},{7,6},{8,9},{9,8},{10,11... | collective-permute-start | bytes 1572872 | tf_op jit(solution)/shard_map/ppermute | solution.py:39
  124.6 0.8 collective-permute-done.9.grad_other
  125.4 3.2 %shard_map.89 = (f32[512,512]{1,0:T(8,128)S(1)}, f32[256,512]{1,0:T(8,128)}, f32[256,512]{1,0:T(8,128)}) custom-call(s32[2]{0:T(128)S(1)} %copy-done.4, f32[256,512]{1,0:T(8,128)S(1)} %add_multiply_fusion.grad_own, f32[256,512]{1,0:T(8,128)S(1)} %collective-permute-done.9.grad_other, f32[256,512]{1,0:T(8,128)S(1)} %get-tuple-element.43.stat_self, ...), custom_call_target="tpu_custom_call" | custom-call | flops 805306368 | bytes 5242880 | tf_op jit(solution)/shard_map/pallas_call | solution.py:200
  128.6 26.6 %shard_map.90.own = f32[512,512]{1,0:T(8,128)S(1)} custom-call(s32[2]{0:T(128)S(1)} %copy-done.4, f32[256,512]{1,0:T(8,128)} %get-tuple-element.37.mine, f32[256,512]{1,0:T(8,128)} %get-tuple-element.38.opposite), custom_call_target="tpu_custom_call" | custom-call | flops 26843545600 | bytes 2097152 | tf_op jit(solution)/shard_map/pallas_call | solution.py:275
  155.6 1.3 collective-permute-start.12
  156.9 5.7 %collective-permute-start.14 = (f32[256,512]{1,0:T(8,128)}, f32[256,512]{1,0:T(8,128)}, u32[]{:S(2)}, u32[]{:S(2)}) collective-permute-start(f32[256,512]{1,0:T(8,128)} %get-tuple-element.37.mine), channel_id=1, source_target_pairs={{1,0},{3,2},{4,5},{6,7},{9,8},{11,10},{12,13},{14,15},{17,16},{19,... | collective-permute-start | bytes 1572872 | tf_op jit(solution)/shard_map/ppermute | solution.py:39
  162.6 2.2 %collective-permute-start.13 = (f32[256,512]{1,0:T(8,128)}, f32[256,512]{1,0:T(8,128)}, u32[]{:S(2)}, u32[]{:S(2)}) collective-permute-start(f32[256,512]{1,0:T(8,128)} %get-tuple-element.38.opposite), channel_id=1, source_target_pairs={{1,4},{3,6},{4,1},{6,3},{9,12},{11,14},{12,9},{14,11},{17,20},{19,... | collective-permute-start | bytes 1572872 | tf_op jit(solution)/shard_map/ppermute | solution.py:39
  164.8 1.3 collective-permute-done.12
  166.2 7.2 %collective-permute-done.13 = f32[256,512]{1,0:T(8,128)} collective-permute-done((f32[256,512]{1,0:T(8,128)}, f32[256,512]{1,0:T(8,128)}, u32[]{:S(2)}, u32[]{:S(2)}) %collective-permute-start.13) | collective-permute-done | bytes 524320 | tf_op jit(solution)/shard_map/ppermute | solution.py:39
  173.4 2.7 %select_select_fusion = (f32[256,512]{1,0:T(8,128)}, f32[256,512]{1,0:T(8,128)}) fusion(f32[256,512]{1,0:T(8,128)} %collective-permute-done.12, f32[256,512]{1,0:T(8,128)} %get-tuple-element.37.mine, f32[256,512]{1,0:T(8,128)} %collective-permute-done.14, f32[256,512]{1,0:T(8,128)} %collective-permute-done.13, pred[]{:T(512)S(6)} %eq.10, pred[]{:T(512)S(6)} %eq.8), kind=kLoop, calls=%fused_computation.1 | loop fusion | flops 786432 | bytes 3145730 | tf_op jit(solution)/shard_map/jit(_where)/select_n | solution.py:366
  176.1 1.7 shard_map.91
  177.8 2.3 %collective-permute-start.11 = (bf16[256,512]{1,0:T(8,128)(2,1)S(1)}, bf16[256,512]{1,0:T(8,128)(2,1)S(1)}, u32[]{:S(2)}, u32[]{:S(2)}) collective-permute-start(bf16[256,512]{1,0:T(8,128)(2,1)S(1)} %shard_map.91), channel_id=1, source_target_pairs={{1,4},{3,6},{4,1},{6,3},{9,12},{11,14},{12,9},{14,11},{17,20},{19,... | collective-permute-start | bytes 786440 | tf_op jit(solution)/shard_map/ppermute | solution.py:39
  180.1 2.8 %add_convert_fusion = bf16[256,2048]{1,0:T(8,128)(2,1)} fusion(f32[256,2048]{1,0:T(8,128)S(1)} %copy-done.5, f32[256,2048]{1,0:T(8,128)} %collective-permute-done.4), kind=kLoop, calls=%fused_computation | loop fusion | flops 1048576 | bytes 5242880 | tf_op jit(solution)/shard_map/convert_element_type | solution.py:369
  183.0 2.5 %collective-permute-done.11 = bf16[256,512]{1,0:T(8,128)(2,1)S(1)} collective-permute-done((bf16[256,512]{1,0:T(8,128)(2,1)S(1)}, bf16[256,512]{1,0:T(8,128)(2,1)S(1)}, u32[]{:S(2)}, u32[]{:S(2)}) %collective-permute-start.11) | collective-permute-done | bytes 262176 | tf_op jit(solution)/shard_map/ppermute | solution.py:39
  (33 shorter events, 5.1 us)
Async XLA Ops:
  8.5 10.0 %copy-start.6 = (bf16[8,256,512]{2,1,0:T(8,128)(2,1)S(1)}, bf16[8,256,512]{2,1,0:T(8,128)(2,1)}, u32[]{:S(2)}) copy-start(bf16[8,256,512]{2,1,0:T(8,128)(2,1)} %get-tuple-element.29) | copy-start | bytes 6291460
  17.2 50.7 %collective-permute-start = (f32[2,256,2048]{2,1,0:T(8,128)}, f32[2,256,2048]{2,1,0:T(8,128)}, u32[]{:S(2)}, u32[]{:S(2)}) collective-permute-start(f32[2,256,2048]{2,1,0:T(8,128)} %shard_map.85), channel_id=1, source_target_pairs={{0,1},{1,0},{2,3},{3,2},{4,5},{5,4},{6,7},{7,6},{8,9},{9,8},{10,11... | collective-permute-start | bytes 12582920 | tf_op jit(solution)/shard_map/ppermute | solution.py:39
  53.7 5.5 %copy-start.7 = (f32[256,512]{1,0:T(8,128)S(1)}, f32[256,512]{1,0:T(8,128)}, u32[]{:S(2)}) copy-start(f32[256,512]{1,0:T(8,128)} %param.9) | copy-start | bytes 1572868
  53.7 36.9 %collective-permute-start.5 = (bf16[2048,512]{1,0:T(8,128)(2,1)S(1)}, bf16[2048,512]{1,0:T(8,128)(2,1)}, u32[]{:S(2)}, u32[]{:S(2)}) collective-permute-start(bf16[2048,512]{1,0:T(8,128)(2,1)S(1)} %bitcast.6), channel_id=1, source_target_pairs={{0,1},{1,0},{2,3},{3,2},{4,5},{5,4},{6,7},{7,6},{8,9},{9,8},{10,11... | collective-permute-start | bytes 6291464 | tf_op jit(solution)/shard_map/ppermute | solution.py:39
  54.8 35.8 %all-to-all-start = ((bf16[8,256,512]{2,1,0:T(8,128)(2,1)}), bf16[8,256,512]{2,1,0:T(8,128)(2,1)}, u32[]{:S(2)}, u32[]{:S(2)}) async-start(bf16[8,256,512]{2,1,0:T(8,128)(2,1)} %get-tuple-element.24), calls=%async_computation | async-start | bytes 4194304 | tf_op jit(solution)/shard_map/all_to_all | solution.py:318
  60.3 18.9 %collective-permute-start.1 = (f32[256,512]{1,0:T(8,128)S(1)}, f32[256,512]{1,0:T(8,128)S(1)}, u32[]{:S(2)}, u32[]{:S(2)}) collective-permute-start(f32[256,512]{1,0:T(8,128)S(1)} %get-tuple-element.43.stat_self), channel_id=1, source_target_pairs={{1,5},{3,7},{4,0},{6,2},{9,13},{11,15},{12,8},{14,10},{17,21},{19,... | collective-permute-start | bytes 1572872 | tf_op jit(solution)/shard_map/ppermute | solution.py:39
  63.6 15.6 %collective-permute-start.2 = (f32[256,512]{1,0:T(8,128)S(1)}, f32[256,512]{1,0:T(8,128)S(1)}, u32[]{:S(2)}, u32[]{:S(2)}) collective-permute-start(f32[256,512]{1,0:T(8,128)S(1)} %get-tuple-element.42), channel_id=1, source_target_pairs={{0,1},{2,3},{5,4},{7,6},{8,9},{10,11},{13,12},{15,14},{16,17},{18,... | collective-permute-start | bytes 1572872 | tf_op jit(solution)/shard_map/ppermute | solution.py:39
  64.9 15.1 %collective-permute-start.3 = (f32[256,512]{1,0:T(8,128)S(1)}, f32[256,512]{1,0:T(8,128)S(1)}, u32[]{:S(2)}, u32[]{:S(2)}) collective-permute-start(f32[256,512]{1,0:T(8,128)S(1)} %get-tuple-element.42), channel_id=1, source_target_pairs={{1,4},{3,6},{4,1},{6,3},{9,12},{11,14},{12,9},{14,11},{17,20},{19,... | collective-permute-start | bytes 1572872 | tf_op jit(solution)/shard_map/ppermute | solution.py:39
  73.5 17.1 %copy-start.4 = (s32[2]{0:T(128)S(1)}, s32[2]{0:T(128)}, u32[]{:S(2)}) copy-start(s32[2]{0:T(128)} %pad_add_fusion.flags) | copy-start | bytes 28
  79.2 0.8 copy-start
  80.0 0.8 copy-start.2
  95.9 29.5 %copy-start.1 = (f32[256,512]{1,0:T(8,128)S(1)}, f32[256,512]{1,0:T(8,128)}, u32[]{:S(2)}) copy-start(f32[256,512]{1,0:T(8,128)} %copy-done) | copy-start | bytes 1572868
  95.9 29.5 %copy-start.3 = (f32[256,512]{1,0:T(8,128)S(1)}, f32[256,512]{1,0:T(8,128)}, u32[]{:S(2)}) copy-start(f32[256,512]{1,0:T(8,128)} %copy-done.2) | copy-start | bytes 1572868
  95.9 25.3 %collective-permute-start.8 = (f32[256,512]{1,0:T(8,128)S(1)}, f32[256,512]{1,0:T(8,128)S(1)}, u32[]{:S(2)}, u32[]{:S(2)}) collective-permute-start(f32[256,512]{1,0:T(8,128)S(1)} %get-tuple-element.33), channel_id=1, source_target_pairs={{0,12},{1,13},{2,14},{3,15},{4,8},{5,9},{6,10},{7,11},{8,4},{9,5},... | collective-permute-start | bytes 1572872 | tf_op jit(solution)/shard_map/ppermute | solution.py:39
  98.7 22.5 %collective-permute-start.7 = (f32[256,512]{1,0:T(8,128)S(1)}, f32[256,512]{1,0:T(8,128)S(1)}, u32[]{:S(2)}, u32[]{:S(2)}) collective-permute-start(f32[256,512]{1,0:T(8,128)S(1)} %get-tuple-element.32), channel_id=1, source_target_pairs={{0,8},{1,9},{2,10},{3,11},{4,12},{5,13},{6,14},{7,15},{8,0},{9,1},... | collective-permute-start | bytes 1572872 | tf_op jit(solution)/shard_map/ppermute | solution.py:39
  99.1 22.5 %collective-permute-start.6 = (f32[256,512]{1,0:T(8,128)S(1)}, f32[256,512]{1,0:T(8,128)S(1)}, u32[]{:S(2)}, u32[]{:S(2)}) collective-permute-start(f32[256,512]{1,0:T(8,128)S(1)} %get-tuple-element.31), channel_id=1, source_target_pairs={{0,4},{1,5},{2,6},{3,7},{4,0},{5,1},{6,2},{7,3},{8,12},{9,13},{10,... | collective-permute-start | bytes 1572872 | tf_op jit(solution)/shard_map/ppermute | solution.py:39
  121.9 3.6 %collective-permute-start.9 = (f32[256,512]{1,0:T(8,128)S(1)}, f32[256,512]{1,0:T(8,128)S(1)}, u32[]{:S(2)}, u32[]{:S(2)}) collective-permute-start(f32[256,512]{1,0:T(8,128)S(1)} %add_multiply_fusion.grad_own), channel_id=1, source_target_pairs={{0,1},{1,0},{2,3},{3,2},{4,5},{5,4},{6,7},{7,6},{8,9},{9,8},{10,11... | collective-permute-start | bytes 1572872 | tf_op jit(solution)/shard_map/ppermute | solution.py:39
  123.9 56.2 %collective-permute-start.4 = (f32[256,2048]{1,0:T(8,128)}, f32[256,2048]{1,0:T(8,128)}, u32[]{:S(2)}, u32[]{:S(2)}) collective-permute-start(f32[256,2048]{1,0:T(8,128)} %shard_map.86), channel_id=1, source_target_pairs={{0,2},{1,3},{2,0},{3,1},{4,6},{5,7},{6,4},{7,5},{8,10},{9,11},{10,... | collective-permute-start | bytes 6291464 | tf_op jit(solution)/shard_map/ppermute | solution.py:39
  155.2 21.0 %collective-permute-start.10 = (f32[512,512]{1,0:T(8,128)S(1)}, f32[512,512]{1,0:T(8,128)S(1)}, u32[]{:S(2)}, u32[]{:S(2)}) collective-permute-start(f32[512,512]{1,0:T(8,128)S(1)} %shard_map.90.own), channel_id=1, source_target_pairs={{0,1},{1,0},{2,3},{3,2},{4,5},{5,4},{6,7},{7,6},{8,9},{9,8},{10,11... | collective-permute-start | bytes 3145736 | tf_op jit(solution)/shard_map/ppermute | solution.py:39
  155.6 10.5 %collective-permute-start.12 = (f32[256,512]{1,0:T(8,128)}, f32[256,512]{1,0:T(8,128)}, u32[]{:S(2)}, u32[]{:S(2)}) collective-permute-start(f32[256,512]{1,0:T(8,128)} %get-tuple-element.38.opposite), channel_id=1, source_target_pairs={{0,4},{2,6},{5,1},{7,3},{8,12},{10,14},{13,9},{15,11},{16,20},{18,... | collective-permute-start | bytes 1572872 | tf_op jit(solution)/shard_map/ppermute | solution.py:39
  156.9 9.2 %collective-permute-start.14 = (f32[256,512]{1,0:T(8,128)}, f32[256,512]{1,0:T(8,128)}, u32[]{:S(2)}, u32[]{:S(2)}) collective-permute-start(f32[256,512]{1,0:T(8,128)} %get-tuple-element.37.mine), channel_id=1, source_target_pairs={{1,0},{3,2},{4,5},{6,7},{9,8},{11,10},{12,13},{14,15},{17,16},{19,... | collective-permute-start | bytes 1572872 | tf_op jit(solution)/shard_map/ppermute | solution.py:39
  162.6 10.8 %collective-permute-start.13 = (f32[256,512]{1,0:T(8,128)}, f32[256,512]{1,0:T(8,128)}, u32[]{:S(2)}, u32[]{:S(2)}) collective-permute-start(f32[256,512]{1,0:T(8,128)} %get-tuple-element.38.opposite), channel_id=1, source_target_pairs={{1,4},{3,6},{4,1},{6,3},{9,12},{11,14},{12,9},{14,11},{17,20},{19,... | collective-permute-start | bytes 1572872 | tf_op jit(solution)/shard_map/ppermute | solution.py:39
  176.1 4.0 %copy-start.5 = (f32[256,2048]{1,0:T(8,128)S(1)}, f32[256,2048]{1,0:T(8,128)}, u32[]{:S(2)}) copy-start(f32[256,2048]{1,0:T(8,128)} %shard_map.87) | copy-start | bytes 6291460
  177.8 7.7 %collective-permute-start.11 = (bf16[256,512]{1,0:T(8,128)(2,1)S(1)}, bf16[256,512]{1,0:T(8,128)(2,1)S(1)}, u32[]{:S(2)}, u32[]{:S(2)}) collective-permute-start(bf16[256,512]{1,0:T(8,128)(2,1)S(1)} %shard_map.91), channel_id=1, source_target_pairs={{1,4},{3,6},{4,1},{6,3},{9,12},{11,14},{12,9},{14,11},{17,20},{19,... | collective-permute-start | bytes 786440 | tf_op jit(solution)/shard_map/ppermute | solution.py:39
